TPU v7x, 512 devices: a whole 4x8x8 slice. The times are simulated.
512 devices in a mesh: ctx: 16 (over z_lo, x, core), exp: 32 (over z_hi, y).
Axes of the slice: x: 4, y: 8, z: 8 (z_hi: 4, z_lo: 2; z = z_hi * 2 + z_lo), core: 2. Of those that a mesh axis runs over, the one named last changes fastest.
Arguments:
- frames_in: bfloat16 [16384, 1536], P(('ctx', 'exp')), may hold values from -6 to 6
- expert_ids: int32 [16384, 2], P(('ctx', 'exp')), may hold values from 0 to 31, all different within a row; in each aligned block of 32 rows (0 to 31, 32 to 63, ...) at most 3 rows name the same one
- gate_values: bfloat16 [16384, 2], P(('ctx', 'exp')), may hold values from 0.19921875 to 1
- norm_gain: float32 [1536], replicated, may hold values from 0.1 to 1.9
- weight_in: bfloat16 [32, 1536, 6144], P('exp', None, 'ctx'), may hold values from -0.15625 to 0.15625
- weight_out: bfloat16 [32, 6144, 1536], P('exp', 'ctx'), may hold values from -0.078125 to 0.078125
Outputs:
- mixed: bfloat16 [16384, 1536], P(('ctx', 'exp'))
Inputs may be any that keep to these rules, and one draw needn't show every extreme that they name: `expert_ids`: the 2 ids of a frame differ. Among the 32 frames of one device (aligned blocks of frames in order) no expert is named more than 3 times, and that count is reached.
All inputs are finite; a program needn't handle non-finite values.
Results may differ from a plain program's by a relative error of at most 0.007.
Values may be sent and summed in bfloat16 or wider, within the bound.
A program may use at most 64 MiB of HBM per device.

v0:
```python
from functools import partial

import jax
import jax.numpy as jnp
from jax import lax
from jax.sharding import Mesh
from jax.sharding import PartitionSpec as P

CTX = ("ctx_0", "ctx_1", "ctx_2")
CTX_EXP = ("ctx_0", "ctx_1", "ctx_2", "exp")


EPSILON = 1e-05


def exchange_in_groups(x, axis, split_dim, concat_dim, work, item_dim, out_dim):
    items = jax.tree.leaves(x)[0].shape[item_dim]
    count = 2 if items % 2 == 0 else 1
    outs = []
    for k in range(count):
        group = jax.tree.map(
            lambda a: lax.slice_in_dim(
                a, k * (items // count), (k + 1) * (items // count), axis=item_dim
            ),
            x,
        )
        outs.append(
            work(
                lax.all_to_all(
                    group, axis, split_axis=split_dim, concat_axis=concat_dim, tiled=True
                )
            )
        )
    return jax.tree.map(lambda *parts: jnp.concatenate(parts, axis=out_dim), *outs)


def laid_out(pieces, dim):
    dims = list(pieces.shape[1:])
    dims[dim] *= pieces.shape[0]
    return jnp.moveaxis(pieces, 0, dim).reshape(dims)


def gather_in_order(x, axes, order):
    pieces = x
    for k in order:
        pieces = lax.all_gather(pieces, axes[k])
    done = order[::-1]
    back = [done.index(k) for k in range(len(axes))]
    pieces = pieces.transpose(*back, *range(len(axes), pieces.ndim))
    return pieces.reshape(-1, *x.shape)


def whole_of(x, axes, order, dim):
    return laid_out(gather_in_order(x, axes, order), dim)


def in_blocks(x, dim, length):
    before, after = (x.shape[:dim], x.shape[dim + 1 :])
    return jnp.moveaxis(x.reshape(*before, length, -1, *after), dim, 0)


def sent_and_summed(x, axis, dim):
    length = lax.axis_size(axis)
    pieces = lax.all_to_all(in_blocks(x, dim, length), axis, 0, 0, tiled=True)
    return jnp.sum(pieces.astype(jnp.float32), axis=0)


def layer_norm(frames, gain):
    values = frames.astype(jnp.float32)
    average = jnp.mean(values, axis=-1, keepdims=True)
    centred = values - average
    variance = jnp.mean(centred * centred, axis=-1, keepdims=True)
    return (centred * lax.rsqrt(variance + EPSILON) * gain).astype(jnp.bfloat16)


def slot_tables(expert_ids, gate_values, experts, capacity):
    frames, width = expert_ids.shape
    flat_ids = expert_ids.reshape(frames * width)
    labels = jnp.arange(experts, dtype=jnp.int32)
    matches = (flat_ids[:, None] == labels[None, :]).astype(jnp.int32)
    earlier = jnp.cumsum(matches, axis=0) - matches
    position = jnp.sum(matches * earlier, axis=1)
    slot_match = (position[:, None] == jnp.arange(capacity, dtype=jnp.int32)[None, :]).astype(
        jnp.float32
    )
    chosen = (matches.astype(jnp.float32)[:, :, None] * slot_match[:, None, :]).reshape(
        frames, width, experts, capacity
    )
    dispatch = jnp.sum(chosen, axis=1)
    weighing = jnp.sum(chosen * gate_values.astype(jnp.float32)[:, :, None, None], axis=1)
    return (dispatch.astype(jnp.bfloat16), weighing.astype(jnp.bfloat16))


def expert_partial(frame_rows, weight_in, weight_out):
    hidden = jnp.einsum(
        "...d,dh->...h", frame_rows, weight_in[0], preferred_element_type=jnp.float32
    )
    activation = (hidden * jax.nn.sigmoid(hidden)).astype(jnp.bfloat16)
    return jnp.einsum(
        "...h,hd->...d", activation, weight_out[0], preferred_element_type=jnp.float32
    ).astype(jnp.bfloat16)


def local(frames_in, expert_ids, gate_values, norm_gain, weight_in, weight_out):
    experts = lax.axis_size("exp")
    frames, selections = expert_ids.shape
    capacity = max(2, 3 * frames * selections // (2 * experts))
    tables = partial(slot_tables, experts=experts, capacity=capacity)
    normed = layer_norm(frames_in, norm_gain)
    own_dispatch = tables(expert_ids, gate_values)[0]
    buffer = jnp.einsum(
        "fes,fd->esd", own_dispatch, normed, preferred_element_type=jnp.float32
    ).astype(jnp.bfloat16)

    def serve_own(received):
        shared = lax.all_gather(received[None], CTX, axis=0, tiled=True)
        return lax.all_to_all(
            expert_partial(shared, weight_in, weight_out),
            "exp",
            split_axis=1,
            concat_axis=1,
            tiled=True,
        )

    partials = exchange_in_groups(buffer, "exp", 0, 0, serve_own, 1, 2)
    group_ids, group_gates = (
        whole_of(expert_ids[None], (("ctx_0", "ctx_1"), "ctx_2"), (0, 1), 0),
        whole_of(gate_values[None], (("ctx_0", "ctx_1"), "ctx_2"), (0, 1), 0),
    )
    weighing = jax.vmap(tables)(group_ids, group_gates)[1]
    combined = jnp.einsum("cfes,cesd->cfd", weighing, partials, preferred_element_type=jnp.float32)
    expert_sum = sent_and_summed(combined.astype(jnp.bfloat16), CTX, 0)
    return (frames_in.astype(jnp.float32) + 0.5 * expert_sum[0]).astype(jnp.bfloat16)


def solution(mesh):
    split = Mesh(
        mesh.devices.reshape(2, 4, 2, mesh.shape["exp"]), ("ctx_0", "ctx_1", "ctx_2", "exp")
    )
    return jax.shard_map(
        local,
        mesh=split,
        in_specs=(
            P(CTX_EXP, None),
            P(CTX_EXP, None),
            P(CTX_EXP, None),
            P(),
            P("exp", None, CTX),
            P("exp", CTX, None),
        ),
        out_specs=P(CTX_EXP, None),
        check_vma=False,
    )
```

profile of v0, /device:TPU:32, one launch (start us, length us, event | category | flops | bytes accessed | tf_op | source)
XLA Modules:
  0.0 320.4 jit_solution(11348033680408547656)
XLA Ops:
  6.5 0.0 copy-start
  6.5 0.0 copy-start.4
  6.5 0.0 all-gather.9.cloned.1.call-start
  6.5 0.9 copy.79
  7.5 0.8 convert_convert_fusion.1
  8.2 0.1 eq.105
  8.3 0.1 fusion.42
  8.4 0.1 reduce_window_sum.23
  8.5 0.2 select_reduce_fusion.1
  8.7 0.1 eq.109
  8.8 0.1 copy.80
  8.9 1.0 convert_reduce_fusion.1
  9.9 1.1 fusion.32
  11.0 0.1 multiply_reduce_fusion.1
  11.1 1.2 convolution_convert_fusion.1
  12.3 0.3 copy.82
  12.6 29.6 %all_to_all.15 = bf16[32,3,1536]{2,1,0:T(4,128)(2,1)S(1)} all-to-all(bf16[32,3,1536]{2,1,0:T(4,128)(2,1)S(1)} %copy.82), channel_id=1, replica_groups=mesh['ctx_0'=2,'ctx_1'=4,'ctx_2'=2,'exp'=32] {'exp'}, dimensions={0} | all-to-all | bytes 589824 | tf_op jit(solution)/shard_map/all_to_all | solution.py:29
  42.2 0.8 copy.83
  43.0 0.0 all-gather.9.cloned.1.call-update
  43.0 40.3 %all-gather.9.cloned.1.call-done = bf16[512,3,1536]{2,0,1:T(8,128)(2,1)} async-done(((bf16[32,3,1536]{2,0,1:T(8,128)(2,1)}), bf16[512,3,1536]{2,0,1:T(8,128)(2,1)}) %all-gather.9.cloned.1.call-update) | async-done | bytes 4718608 | tf_op jit(solution)/shard_map/all_gather | solution.py:116
  83.3 0.0 copy-done
  83.3 0.0 copy-done.4
  83.3 8.4 %convolution_convert_fusion = bf16[16,32,3,1536]{3,1,2,0:T(8,128)(2,1)} fusion(bf16[1,384,1536]{2,1,0:T(8,128)(2,1)S(1)} %copy-done, bf16[16,32,3,1536]{3,1,0,2:T(8,128)(2,1)} %bitcast.67, bf16[1,1536,384]{2,1,0:T(8,128)(2,1)S(1)} %copy-done.4), kind=kOutput, calls=%fused_computation.4 | convolution fusion | flops 3629187072 | bytes 11796480 | tf_op jit(solution)/shard_map/...h,hd->...d/dot_general | solution.py:99
  91.8 7.0 %copy.85 = bf16[16,32,3,1536]{3,0,2,1:T(8,128)(2,1)} copy(bf16[16,32,3,1536]{3,1,2,0:T(8,128)(2,1)} %convolution_convert_fusion) | data formatting | bytes 9437184 | tf_op jit(solution)/shard_map/convert_element_type | solution.py:101
  98.8 0.0 copy-start.2
  98.8 0.0 copy-start.3
  98.8 12.6 %all-to-all-start.1 = ((bf16[16,32,3,1536]{3,0,2,1:T(8,128)(2,1)}), bf16[16,32,3,1536]{3,0,2,1:T(8,128)(2,1)}, u32[]{:S(2)}, u32[]{:S(2)}) async-start(bf16[16,32,3,1536]{3,0,2,1:T(8,128)(2,1)} %copy.85), calls=%async_computation.1 | async-start | bytes 9437184 | tf_op jit(solution)/shard_map/all_to_all | solution.py:117
  111.4 0.0 copy-done.2
  111.4 93.1 %all-gather.5 = s32[8,32,2]{1,2,0:T(2,128)S(1)} all-gather(s32[1,32,2]{1,2,0:T(2,128)S(1)} %bitcast.65), channel_id=2, replica_groups=mesh['ctx_0'=2,'ctx_1'=4,'ctx_2'=2,'exp'=32] {'ctx_0','ctx_1'}, dimensions={0}, use_global_device_ids=true | all-gather | bytes 2304 | tf_op jit(solution)/shard_map/all_gather | solution.py:46
  204.6 1.8 all-gather.1
  206.4 0.2 copy.71
  206.5 0.2 copy.73
  206.7 0.2 eq.94
  206.9 0.1 copy.74
  207.0 1.4 select_reduce_fusion
  208.4 0.1 copy.75
  208.5 0.0 copy-done.3
  208.5 15.1 %all-gather.6 = bf16[8,32,2]{1,2,0:T(2,128)(2,1)S(1)} all-gather(bf16[1,32,2]{1,2,0:T(2,128)(2,1)S(1)} %bitcast.66), channel_id=4, replica_groups=mesh['ctx_0'=2,'ctx_1'=4,'ctx_2'=2,'exp'=32] {'ctx_0','ctx_1'}, dimensions={0}, use_global_device_ids=true | all-gather | bytes 1152 | tf_op jit(solution)/shard_map/all_gather | solution.py:46
  223.6 2.0 all-gather.3
  225.6 0.2 convert_convert_fusion
  225.8 0.8 multiply_reduce_fusion
  226.6 44.4 %all-to-all-done.1 = bf16[16,32,3,1536]{3,0,2,1:T(8,128)(2,1)} async-done(((bf16[16,32,3,1536]{3,0,2,1:T(8,128)(2,1)}), bf16[16,32,3,1536]{3,0,2,1:T(8,128)(2,1)}, u32[]{:S(2)}, u32[]{:S(2)}) %all-to-all-start.1) | async-done | bytes 4718624 | tf_op jit(solution)/shard_map/all_to_all | solution.py:117
  271.0 7.8 %fusion.10 = bf16[16,1,32,1536]{3,2,1,0:T(8,128)(2,1)S(1)} fusion(bf16[16,32,3,1536]{3,0,2,1:T(8,128)(2,1)} %all-to-all-done.1, bf16[16,32,32,3]{2,1,3,0:T(8,128)(2,1)S(1)} %multiply_reduce_fusion), kind=kOutput, calls=%fused_computation.8 | convolution fusion | flops 151781376 | bytes 6389760 | tf_op jit(solution)/shard_map/cfes,cesd->cfd/dot_general | solution.py:131
  278.9 0.0 copy-start.1
  278.9 33.7 %all_to_all.16 = bf16[16,1,32,1536]{3,2,1,0:T(8,128)(2,1)S(1)} all-to-all(bf16[16,1,32,1536]{3,2,1,0:T(8,128)(2,1)S(1)} %fusion.10), channel_id=1, replica_groups=mesh['ctx_0'=2,'ctx_1'=4,'ctx_2'=2,'exp'=32] {'ctx_0','ctx_1','ctx_2'}, dimensions={0} | all-to-all | bytes 3145728 | tf_op jit(solution)/shard_map/all_to_all | solution.py:64
  312.6 0.2 convert_reduce_fusion
  312.9 0.0 copy-done.1
  312.9 0.7 fusion.35
  (6 shorter events, 0.1 us)
Async XLA Ops:
  6.5 76.8 %copy-start = (bf16[1,384,1536]{2,1,0:T(8,128)(2,1)S(1)}, bf16[1,384,1536]{2,1,0:T(8,128)(2,1)}, u32[]{:S(2)}) copy-start(bf16[1,384,1536]{2,1,0:T(8,128)(2,1)} %param.11) | copy-start | bytes 3538948
  6.5 76.8 %copy-start.4 = (bf16[1,1536,384]{2,1,0:T(8,128)(2,1)S(1)}, bf16[1,1536,384]{2,1,0:T(8,128)(2,1)}, u32[]{:S(2)}) copy-start(bf16[1,1536,384]{2,1,0:T(8,128)(2,1)} %param.10) | copy-start | bytes 3538948
  6.5 76.8 %all-gather.9.cloned.1.call-start = ((), (), s32[]{:S(2)}) async-start(), calls=%async_computation.3 | async-start | bytes 5013504 | tf_op jit(solution)/shard_map/all_gather | solution.py:116
  98.8 12.6 %copy-start.2 = (s32[32,2]{0,1:T(2,128)S(1)}, s32[32,2]{0,1:T(2,128)}, u32[]{:S(2)}) copy-start(s32[32,2]{0,1:T(2,128)} %param.7) | copy-start | bytes 772
  98.8 109.7 %copy-start.3 = (bf16[32,2]{0,1:T(2,128)(2,1)S(1)}, bf16[32,2]{0,1:T(2,128)(2,1)}, u32[]{:S(2)}) copy-start(bf16[32,2]{0,1:T(2,128)(2,1)} %param.8) | copy-start | bytes 388
  98.8 172.2 %all-to-all-start.1 = ((bf16[16,32,3,1536]{3,0,2,1:T(8,128)(2,1)}), bf16[16,32,3,1536]{3,0,2,1:T(8,128)(2,1)}, u32[]{:S(2)}, u32[]{:S(2)}) async-start(bf16[16,32,3,1536]{3,0,2,1:T(8,128)(2,1)} %copy.85), calls=%async_computation.1 | async-start | bytes 9437184 | tf_op jit(solution)/shard_map/all_to_all | solution.py:117
  278.9 34.0 %copy-start.1 = (bf16[32,1536]{1,0:T(8,128)(2,1)S(1)}, bf16[32,1536]{1,0:T(8,128)(2,1)}, u32[]{:S(2)}) copy-start(bf16[32,1536]{1,0:T(8,128)(2,1)} %param.6) | copy-start | bytes 294916
Sparse Core Ops, SparseCore 0:
  43.1 40.1 all-gather.8
where the time goes:
time: 321 us; the launch traced here: 320 us
  blocking collectives  175 us (55%)
  waiting for transfers between devices  84.7 us (26%)
  matrix products  17.5 us (5%)
  between operations  13.5 us (4%)
  starting transfers between devices  12.6 us (4%)
  local copies, waits for them, and re-layouts  9.98 us (3%)
  other arithmetic  6.7 us (2%)
    all_gather x4, blocking collectives, gather_in_order(): pieces = lax.all_gather(pieces, axes[k])  112 us
    all_to_all x1, waiting for transfers between devices, serve_own(): lax.all_to_all(expert_partial(shared, weight_in, weight_out), 'exp', spli...  44.4 us
    all_gather x1, waiting for transfers between devices, serve_own(): shared = lax.all_gather(received[None], CTX, axis=0, tiled=True)  40.3 us
    all_to_all x1, blocking collectives, sent_and_summed(): pieces = lax.all_to_all(in_blocks(x, dim, length), axis, 0, 0, tiled=True)  33.7 us
    all_to_all x1, blocking collectives, exchange_in_groups(): lax.all_to_all(group, axis, split_axis=split_dim, concat_axis=concat_dim,...  29.6 us
    all_to_all x1, starting transfers between devices, serve_own(): lax.all_to_all(expert_partial(shared, weight_in, weight_out), 'exp', spli...  12.6 us
    dot_general x1, matrix products, expert_partial(): jnp.einsum('...h,hd->...d', activation, weight_out[0], preferred_element_...  8.45 us
    dot_general x1, matrix products, local(): jnp.einsum('cfes,cesd->cfd', weighing, partials, preferred_element_type=j...  7.84 us
  transfers between devices with their start and end apart: 2, of which 2 were waited for; matrix products, arithmetic and copies ran while one was open for 1% of the time, Pallas kernels for 0%

commit v1 on v0

--- a/solution.py
+++ b/solution.py
@@ -105,32 +105,20 @@
     experts = lax.axis_size("exp")
     frames, selections = expert_ids.shape
     capacity = max(2, 3 * frames * selections // (2 * experts))
-    tables = partial(slot_tables, experts=experts, capacity=capacity)
     normed = layer_norm(frames_in, norm_gain)
-    own_dispatch = tables(expert_ids, gate_values)[0]
+    dispatch, weighing = slot_tables(expert_ids, gate_values, experts, capacity)
     buffer = jnp.einsum(
-        "fes,fd->esd", own_dispatch, normed, preferred_element_type=jnp.float32
+        "fes,fd->esd", dispatch, normed, preferred_element_type=jnp.float32
     ).astype(jnp.bfloat16)
-
-    def serve_own(received):
-        shared = lax.all_gather(received[None], CTX, axis=0, tiled=True)
-        return lax.all_to_all(
-            expert_partial(shared, weight_in, weight_out),
-            "exp",
-            split_axis=1,
-            concat_axis=1,
-            tiled=True,
-        )
-
-    partials = exchange_in_groups(buffer, "exp", 0, 0, serve_own, 1, 2)
-    group_ids, group_gates = (
-        whole_of(expert_ids[None], (("ctx_0", "ctx_1"), "ctx_2"), (0, 1), 0),
-        whole_of(gate_values[None], (("ctx_0", "ctx_1"), "ctx_2"), (0, 1), 0),
+    received = lax.all_to_all(buffer, "exp", split_axis=0, concat_axis=0, tiled=True)
+    shared = lax.all_gather(received.reshape(experts * capacity, -1), CTX, axis=0, tiled=True)
+    partials = expert_partial(shared, weight_in, weight_out)
+    summed = lax.psum_scatter(partials, CTX, scatter_dimension=0, tiled=True)
+    back = lax.all_to_all(
+        summed.reshape(experts, capacity, -1), "exp", split_axis=0, concat_axis=0, tiled=True
     )
-    weighing = jax.vmap(tables)(group_ids, group_gates)[1]
-    combined = jnp.einsum("cfes,cesd->cfd", weighing, partials, preferred_element_type=jnp.float32)
-    expert_sum = sent_and_summed(combined.astype(jnp.bfloat16), CTX, 0)
-    return (frames_in.astype(jnp.float32) + 0.5 * expert_sum[0]).astype(jnp.bfloat16)
+    expert_sum = jnp.einsum("fes,esd->fd", weighing, back, preferred_element_type=jnp.float32)
+    return (frames_in.astype(jnp.float32) + 0.5 * expert_sum).astype(jnp.bfloat16)
 
 
 def solution(mesh):

time: 321 us -> 203 us (0.63)
  the two profiles are of different devices: /device:TPU:32 before, /device:TPU:8 now
where the time goes in v1:
time: 203 us
  waiting for transfers between devices  111 us (55%)
  blocking collectives  60.3 us (30%)
  between operations  13.5 us (7%)
  matrix products  10.5 us (5%)
  other arithmetic  4.02 us (2%)
  local copies, waits for them, and re-layouts  3.54 us (2%)
    reduce_scatter x1, waiting for transfers between devices, local(): summed = lax.psum_scatter(partials, CTX, scatter_dimension=0, tiled=True)  73.9 us
    all_gather x1, waiting for transfers between devices, local(): lax.all_gather(received.reshape(experts * capacity, -1), CTX, axis=0, til...  36.8 us
    all_to_all x1, blocking collectives, local(): lax.all_to_all(buffer, 'exp', split_axis=0, concat_axis=0, tiled=True)  33.3 us
    all_to_all x1, blocking collectives, local(): lax.all_to_all(summed.reshape(experts, capacity, -1), 'exp', split_axis=0...  27 us
    dot_general x1, matrix products, expert_partial(): jnp.einsum('...h,hd->...d', activation, weight_out[0], preferred_element_...  8.42 us
  transfers between devices with their start and end apart: 2, of which 2 were waited for; matrix products, arithmetic and copies ran while one was open for 0% of the time, Pallas kernels for 0%

profile of v1, /device:TPU:8, one launch (start us, length us, event | category | flops | bytes accessed | tf_op | source)
XLA Modules:
  0.0 202.6 jit_solution(6943709375496778555)
XLA Ops:
  6.5 0.0 copy-start
  6.5 0.0 copy-start.2
  6.5 0.0 all-gather.2.cloned.1.call-start
  6.5 0.9 copy.21
  7.5 0.8 convert_convert_fusion
  8.2 1.0 convert_reduce_fusion
  9.2 1.1 fusion.14
  10.3 0.7 convert_element_type.56
  11.0 0.1 eq.47
  11.1 0.1 fusion.23
  11.2 0.1 reduce_window_sum.11
  11.3 0.2 select_reduce_fusion
  11.5 0.1 eq.51
  11.6 0.1 copy.22
  11.7 0.1 fusion.17
  11.8 1.2 convolution_convert_fusion.1
  13.0 0.3 copy.24
  13.2 33.3 %all_to_all.10 = bf16[32,3,1536]{2,1,0:T(4,128)(2,1)S(1)} all-to-all(bf16[32,3,1536]{2,1,0:T(4,128)(2,1)S(1)} %copy.24), channel_id=1, replica_groups=mesh['ctx_0'=2,'ctx_1'=4,'ctx_2'=2,'exp'=32] {'exp'}, dimensions={0} | all-to-all | bytes 589824 | tf_op jit(solution)/shard_map/all_to_all | solution.py:113
  46.6 1.0 reshape.67
  47.5 0.0 all-gather.2.cloned.1.call-update
  47.6 0.0 reduce-scatter.2.cloned.1.call-start
  47.6 36.8 %all-gather.2.cloned.1.call-done = bf16[1536,1536]{1,0:T(8,128)(2,1)} async-done(((bf16[96,1536]{1,0:T(8,128)(2,1)}), bf16[1536,1536]{1,0:T(8,128)(2,1)}) %all-gather.2.cloned.1.call-update) | async-done | bytes 4718608 | tf_op jit(solution)/shard_map/all_gather | solution.py:114
  84.5 0.0 copy-done
  84.5 0.0 copy-done.2
  84.5 8.4 %convolution_convert_fusion = bf16[1536,1536]{1,0:T(8,128)(2,1)} fusion(bf16[1,384,1536]{2,1,0:T(8,128)(2,1)S(1)} %copy-done, bf16[1536,1536]{1,0:T(8,128)(2,1)} %all-gather.2.cloned.1.call-done, bf16[1,1536,384]{2,1,0:T(8,128)(2,1)S(1)} %copy-done.2), kind=kOutput, calls=%fused_computation | convolution fusion | flops 3629187072 | bytes 11796480 | tf_op jit(solution)/shard_map/...h,hd->...d/dot_general | solution.py:99
  92.9 0.0 copy-start.1
  92.9 0.0 reduce-scatter.2.cloned.1.call-update
  92.9 73.9 %reduce-scatter.2.cloned.1.call-done = bf16[96,1536]{1,0:T(8,128)(2,1)} async-done(((bf16[1536,1536]{1,0:T(8,128)(2,1)}), bf16[96,1536]{1,0:T(8,128)(2,1)}) %reduce-scatter.2.cloned.1.call-update) | async-done | bytes 294928 | tf_op jit(solution)/shard_map/reduce_scatter | solution.py:116
  166.8 1.1 reshape.68
  167.9 27.0 %all_to_all.11 = bf16[32,3,1536]{2,1,0:T(4,128)(2,1)S(1)} all-to-all(bf16[32,3,1536]{2,1,0:T(4,128)(2,1)S(1)} %reshape.68), channel_id=1, replica_groups=mesh['ctx_0'=2,'ctx_1'=4,'ctx_2'=2,'exp'=32] {'exp'}, dimensions={0} | all-to-all | bytes 589824 | tf_op jit(solution)/shard_map/all_to_all | solution.py:117
  194.9 0.0 copy-done.1
  194.9 0.9 fusion.2
  (3 shorter events, 0.0 us)
Async XLA Ops:
  6.5 77.9 %copy-start = (bf16[1,384,1536]{2,1,0:T(8,128)(2,1)S(1)}, bf16[1,384,1536]{2,1,0:T(8,128)(2,1)}, u32[]{:S(2)}) copy-start(bf16[1,384,1536]{2,1,0:T(8,128)(2,1)} %param.11) | copy-start | bytes 3538948
  6.5 77.9 %copy-start.2 = (bf16[1,1536,384]{2,1,0:T(8,128)(2,1)S(1)}, bf16[1,1536,384]{2,1,0:T(8,128)(2,1)}, u32[]{:S(2)}) copy-start(bf16[1,1536,384]{2,1,0:T(8,128)(2,1)} %param.10) | copy-start | bytes 3538948
  6.5 77.9 %all-gather.2.cloned.1.call-start = ((), (), s32[]{:S(2)}) async-start(), calls=%async_computation.3 | async-start | bytes 5013504 | tf_op jit(solution)/shard_map/all_gather | solution.py:114
  47.6 119.2 %reduce-scatter.2.cloned.1.call-start = ((), (), s32[]{:S(2)}) async-start(), calls=%async_computation.4 | async-start | bytes 5013504 | tf_op jit(solution)/shard_map/reduce_scatter | solution.py:116
  92.9 102.0 %copy-start.1 = (bf16[32,1536]{1,0:T(8,128)(2,1)S(1)}, bf16[32,1536]{1,0:T(8,128)(2,1)}, u32[]{:S(2)}) copy-start(bf16[32,1536]{1,0:T(8,128)(2,1)} %param.6) | copy-start | bytes 294916
Sparse Core Ops, SparseCore 0:
  47.7 36.7 all-gather.1
  93.0 73.6 reduce-scatter.1
